TPU v7x, 256 devices: a whole 4x4x8 slice. The times are simulated.
256 devices in a mesh: gx: 32 (over x, z_hi, core), sec: 8 (over z_lo, y).
Axes of the slice: x: 4, y: 4, z: 8 (z_hi: 4, z_lo: 2; z = z_hi * 2 + z_lo), core: 2. Of those that a mesh axis runs over, the one named last changes fastest.
Arguments:
- state_init: float32 [16, 256, 64, 128], P(None, 'gx', 'sec'), may hold values from -6 to 6
- rock_type: int32 [256, 4096], P('gx', 'sec'), may hold values from 0 to 15
- perm_table: float32 [3, 16], replicated, may hold values from 0.2 to 1
- well_cells: int32 [256], replicated, may hold values from 0 to 1048575
- well_rate: float32 [16, 256], replicated, may hold values from -12 to 12
- basis_in: bfloat16 [256, 64, 128, 256], P(('gx', 'sec')), may hold values from -4 to 4
- singular: float32 [256], replicated, may hold values from 0.5 to 2
Outputs:
- state_out: float32 [16, 256, 64, 128], P(None, 'gx', 'sec')
- basis_out: bfloat16 [256, 64, 128, 256], P(('gx', 'sec'))
- singular_out: float32 [256], replicated
All inputs are finite; a program needn't handle non-finite values.
Results may differ from a plain program's by a relative error of at most 0.0059.
Values may be sent and summed in bfloat16 or wider, within the bound.
A program may use at most 128 MiB of HBM per device.

v0:
```python
import jax
import jax.numpy as jnp
from jax import lax
from jax.sharding import PartitionSpec as P

MG = 8
STEPS = 4
GROUPS = 2
DT_PRESSURE = 0.12
DT_SATURATION = 0.06
DT_ADVECT = 0.15


def with_halo(block, sides, width):
    for axis, dim in sides:
        count = lax.axis_size(axis)
        forward = [(i, i + 1) for i in range(count - 1)]
        backward = [(target, source) for source, target in forward]
        low = lax.ppermute(
            lax.slice_in_dim(block, block.shape[dim] - width, None, axis=dim), axis, forward
        )
        high = lax.ppermute(lax.slice_in_dim(block, 0, width, axis=dim), axis, backward)
        block = jnp.concatenate([low, block, high], axis=dim)
    return block


def harmonic(left, right):
    return 2.0 * left * right / (left + right)


def shift_layers(fields):
    blank = jnp.zeros_like(fields[..., :1])
    return (
        jnp.concatenate([fields[..., 1:], blank], -1),
        jnp.concatenate([blank, fields[..., :-1]], -1),
    )


def advance(fields, besides, weights, inflow, layers):
    column = lax.broadcasted_iota(jnp.int32, (fields.shape[-1],), 0)
    step_sizes = jnp.where(column < layers, DT_PRESSURE, DT_SATURATION)
    is_sat = (column >= layers).astype(fields.dtype)
    press_both = jnp.concatenate([fields[..., :layers], fields[..., :layers]], -1)
    spread = jnp.zeros_like(fields)
    carried = jnp.zeros_like(fields)
    for beside, weight in zip(besides, weights):
        spread = spread + weight * (beside - fields)
        beside_press = jnp.concatenate([beside[..., :layers], beside[..., :layers]], -1)
        pushed = weight * (beside_press - press_both)
        carried = carried + jnp.maximum(pushed, 0.0) * beside + jnp.minimum(pushed, 0.0) * fields
    return fields + step_sizes * spread + DT_ADVECT * is_sat * carried + DT_PRESSURE * inflow


HIGH = lax.Precision.HIGHEST


def hdot(a, b):
    return jnp.dot(a, b, precision=HIGH)


def batch_update(coeffs, gram_of, sigma):
    rounded = coeffs.astype(jnp.bfloat16).astype(jnp.float32)
    gram = gram_of(coeffs, rounded)
    square = jnp.diag(sigma * sigma)
    total = square + hdot(coeffs.T, coeffs)
    inner = hdot(total, total) + hdot(coeffs.T, hdot(gram, coeffs))
    factor = jnp.linalg.cholesky(inner)
    eye = jnp.eye(sigma.shape[0], dtype=jnp.float32)
    back = lax.linalg.triangular_solve(factor, eye, left_side=True, lower=True).T
    top = sigma[:, None] * hdot(total, back)
    bottom = hdot(hdot(coeffs, total) + hdot(gram, coeffs), back)
    sigma_next = jnp.sqrt(jnp.sum(top * top, axis=0) + jnp.sum(bottom * bottom, axis=0))
    on_basis = hdot(square + hdot((coeffs - rounded).T, coeffs), back)
    on_snaps = hdot(coeffs, back)
    return (on_basis, on_snaps, sigma_next)


def small_algebra(uu, su, ss, sigma):
    half = su.shape[0] // 2
    s00, s10, s11 = (ss[:half, :half], ss[half:, :half], ss[half:, half:])

    def gram_first(c, r):
        cr = hdot(c, r.T)
        return s00 - cr - cr.T + hdot(r, hdot(uu, r.T))

    wu, ws, sigma1 = batch_update(su[:half], gram_first, sigma)
    coeffs1 = hdot(su[half:], wu) + hdot(s10, ws)

    def gram_second(c, r):
        cr = hdot(c, r.T)
        yu, ys = (hdot(wu, r.T), hdot(ws, r.T))
        mixed = hdot(ys.T, hdot(su[:half], yu))
        own = hdot(yu.T, hdot(uu, yu)) + mixed + mixed.T + hdot(ys.T, hdot(s00, ys))
        return s11 - cr - cr.T + own

    wu1, ws1, sigma2 = batch_update(coeffs1, gram_second, sigma1)
    return (hdot(wu, wu1), hdot(ws, wu1), ws1, sigma2)


def body(state_init, rock_type, perm_table, well_cells, well_rate, basis_in, singular):
    across = state_init.shape[1]
    along = state_init.shape[2]
    layers = state_init.shape[3] // 2
    sec_count = lax.axis_size("sec")
    rock_count = perm_table.shape[1]
    kinds = lax.broadcasted_iota(jnp.int32, (rock_count, 1, 1), 0)
    picks = (rock_type[None] == kinds).astype(jnp.float32)
    perm = jnp.einsum("dr,rxc->dxc", perm_table, picks, precision=lax.Precision.HIGHEST).reshape(
        3, across, along, layers
    )
    paired = jnp.concatenate([perm[0], perm[1]], -1)
    bordered_perm = with_halo(paired.astype(jnp.bfloat16), (("gx", 0), ("sec", 1)), 1).astype(
        paired.dtype
    )
    perm_xh = bordered_perm[..., :layers]
    perm_yh = bordered_perm[..., layers:]
    x_up = harmonic(perm[0], perm_xh[2:, 1:-1])
    x_down = harmonic(perm_xh[:-2, 1:-1], perm[0])
    y_up = harmonic(perm[1], perm_yh[1:-1, 2:])
    y_down = harmonic(perm_yh[1:-1, :-2], perm[1])
    z_padded = jnp.pad(perm[2], ((0, 0), (0, 0), (1, 1)))
    z_up = harmonic(perm[2], z_padded[..., 2:])
    z_down = harmonic(z_padded[..., :-2], perm[2])
    weights = [
        jnp.concatenate([face, face], -1) for face in (x_up, x_down, y_up, y_down, z_up, z_down)
    ]
    x_start = lax.axis_index("gx") * across
    y_start = lax.axis_index("sec") * along
    total_y = along * sec_count
    x_pos = lax.broadcasted_iota(jnp.int32, (across, along, layers), 0)
    y_pos = lax.broadcasted_iota(jnp.int32, (across, along, layers), 1)
    z_pos = lax.broadcasted_iota(jnp.int32, (across, along, layers), 2)
    cell_ids = ((x_start + x_pos) * total_y + y_start + y_pos) * layers + z_pos
    hits = (well_cells[:, None] == cell_ids.reshape(1, -1)).astype(jnp.float32)
    source = jnp.dot(well_rate, hits, precision=lax.Precision.HIGHEST).reshape(
        state_init.shape[0], across, along, layers
    )
    source_full = jnp.concatenate([source, jnp.zeros_like(source)], -1)
    local_rows = basis_in.shape[0] * basis_in.shape[1] * basis_in.shape[2]
    rows_total = local_rows * lax.axis_size("gx") * sec_count
    finals = []
    snaps = []
    for group in range(GROUPS):
        fields = state_init[group * MG : (group + 1) * MG]
        inflow = source_full[group * MG : (group + 1) * MG]
        saved = []
        for step_index in range(STEPS):
            bordered = with_halo(fields.astype(jnp.bfloat16), (("gx", 1), ("sec", 2)), 1).astype(
                fields.dtype
            )
            up_layer, down_layer = shift_layers(fields)
            besides = [
                bordered[:, 2:, 1:-1],
                bordered[:, :-2, 1:-1],
                bordered[:, 1:-1, 2:],
                bordered[:, 1:-1, :-2],
                up_layer,
                down_layer,
            ]
            fields = advance(fields, besides, weights, inflow, layers)
            snapshot = fields.astype(jnp.bfloat16)
            saved.append(snapshot)
        finals.append(fields)
        stacked = jnp.concatenate(saved, 0)
        stacked = lax.all_to_all(stacked, "sec", split_axis=1, concat_axis=2, tiled=True)
        snaps.append(stacked.reshape(stacked.shape[0], -1))
    both = jnp.concatenate(snaps, 0)
    basis = basis_in.reshape(both.shape[1], basis_in.shape[-1])
    count = basis.shape[1]
    uu = lax.dot_general(basis, basis, (((0,), (0,)), ((), ())), preferred_element_type=jnp.float32)
    su = jnp.dot(both, basis, preferred_element_type=jnp.float32)
    ss = lax.dot_general(both, both, (((1,), (1,)), ((), ())), preferred_element_type=jnp.float32)
    local = jnp.concatenate(
        [
            jnp.concatenate([uu, su], 0),
            jnp.pad(
                jnp.concatenate([jnp.zeros((count, both.shape[0]), jnp.float32), ss], 0),
                ((0, 0), (0, 64)),
            ),
        ],
        1,
    )
    whole = lax.psum(local, ("gx", "sec")) / rows_total
    w0, w1, w2, sigma = small_algebra(
        whole[:count, :count],
        whole[count:, :count],
        whole[count:, count : count + both.shape[0]],
        singular,
    )
    fresh = jnp.dot(basis, w0.astype(jnp.bfloat16), preferred_element_type=jnp.float32)
    fresh = fresh + lax.dot_general(
        both,
        jnp.concatenate([w1, w2], 0).astype(jnp.bfloat16),
        (((0,), (0,)), ((), ())),
        preferred_element_type=jnp.float32,
    )
    basis_now = fresh.astype(jnp.bfloat16).reshape(basis_in.shape)
    return (jnp.concatenate(finals, 0), basis_now, sigma)


def solution(mesh):
    return jax.shard_map(
        body,
        mesh=mesh,
        in_specs=(
            P(None, "gx", "sec", None),
            P("gx", "sec"),
            P(),
            P(),
            P(),
            P(("gx", "sec"), None, None, None),
            P(),
        ),
        out_specs=(P(None, "gx", "sec", None), P(("gx", "sec"), None, None, None), P()),
        check_vma=False,
    )
```

profile of v0, /device:TPU:6, one launch (start us, length us, event | category | flops | bytes accessed | tf_op | source)
XLA Modules:
  0.0 627.0 jit_solution(13930910843129405325)
XLA Ops:
  11.1 7.9 %collective-permute-start.1 = (bf16[1,8,128]{2,1,0:T(8,128)(2,1)}, bf16[1,8,128]{2,1,0:T(8,128)(2,1)}, u32[]{:S(2)}, u32[]{:S(2)}) collective-permute-start(bf16[1,8,128]{2,1,0:T(8,128)(2,1)} %get-tuple-element.186), channel_id=1, source_target_pairs={{8,0},{16,8},{24,16},{32,24},{40,32},{48,40},{56,48},{64,56},{72,6... | collective-permute-start | bytes 6152 | tf_op jit(solution)/shard_map/ppermute | solution.py:22
  22.6 6.7 %collective-permute-start.5 = (bf16[8,1,8,128]{3,2,0,1:T(8,128)(2,1)}, bf16[8,1,8,128]{3,2,0,1:T(8,128)(2,1)}, u32[]{:S(2)}, u32[]{:S(2)}) collective-permute-start(bf16[8,1,8,128]{3,2,0,1:T(8,128)(2,1)} %get-tuple-element.160), channel_id=1, source_target_pairs={{8,0},{16,8},{24,16},{32,24},{40,32},{48,40},{56,48},{64,56},{72,6... | collective-permute-start | bytes 49160 | tf_op jit(solution)/shard_map/ppermute | solution.py:22
  34.6 5.5 fusion.8
  51.2 6.4 %collective-permute-start.21 = (bf16[8,1,8,128]{3,2,0,1:T(8,128)(2,1)}, bf16[8,1,8,128]{3,2,0,1:T(8,128)(2,1)S(1)}, u32[]{:S(2)}, u32[]{:S(2)}) collective-permute-start(bf16[8,1,8,128]{3,2,0,1:T(8,128)(2,1)} %get-tuple-element.168), channel_id=1, source_target_pairs={{8,0},{16,8},{24,16},{32,24},{40,32},{48,40},{56,48},{64,56},{72,6... | collective-permute-start | bytes 49160 | tf_op jit(solution)/shard_map/ppermute | solution.py:22
  59.5 4.3 collective-permute-start.6
  65.2 4.5 collective-permute-start.22
  79.1 6.7 %collective-permute-start.9 = (bf16[8,1,8,128]{3,2,0,1:T(8,128)(2,1)S(1)}, bf16[8,1,8,128]{3,2,0,1:T(8,128)(2,1)S(1)}, u32[]{:S(2)}, u32[]{:S(2)}) collective-permute-start(bf16[8,1,8,128]{3,2,0,1:T(8,128)(2,1)S(1)} %get-tuple-element.158), channel_id=1, source_target_pairs={{8,0},{16,8},{24,16},{32,24},{40,32},{48,40},{56,48},{64,56},{72,6... | collective-permute-start | bytes 49160 | tf_op jit(solution)/shard_map/ppermute | solution.py:22
  87.9 6.7 %collective-permute-start.25 = (bf16[8,1,8,128]{3,2,0,1:T(8,128)(2,1)S(1)}, bf16[8,1,8,128]{3,2,0,1:T(8,128)(2,1)S(1)}, u32[]{:S(2)}, u32[]{:S(2)}) collective-permute-start(bf16[8,1,8,128]{3,2,0,1:T(8,128)(2,1)S(1)} %get-tuple-element.166), channel_id=1, source_target_pairs={{8,0},{16,8},{24,16},{32,24},{40,32},{48,40},{56,48},{64,56},{72,6... | collective-permute-start | bytes 49160 | tf_op jit(solution)/shard_map/ppermute | solution.py:22
  99.7 6.7 %collective-permute-start.26 = (bf16[8,10,1,128]{3,2,0,1:T(2,128)(2,1)S(1)}, bf16[8,10,1,128]{3,2,0,1:T(2,128)(2,1)S(1)}, u32[]{:S(2)}, u32[]{:S(2)}) collective-permute-start(bf16[8,10,1,128]{3,2,0,1:T(2,128)(2,1)S(1)} %get-tuple-element.149), channel_id=1, source_target_pairs={{0,1},{1,2},{2,3},{3,4},{4,5},{5,6},{6,7},{8,9},{9,10},{10,11},{11... | collective-permute-start | bytes 61448 | tf_op jit(solution)/shard_map/ppermute | solution.py:19
  109.5 4.9 collective-permute-done.27
  117.9 6.7 %collective-permute-start.13 = (bf16[8,1,8,128]{3,2,0,1:T(8,128)(2,1)S(1)}, bf16[8,1,8,128]{3,2,0,1:T(8,128)(2,1)S(1)}, u32[]{:S(2)}, u32[]{:S(2)}) collective-permute-start(bf16[8,1,8,128]{3,2,0,1:T(8,128)(2,1)S(1)} %get-tuple-element.156), channel_id=1, source_target_pairs={{8,0},{16,8},{24,16},{32,24},{40,32},{48,40},{56,48},{64,56},{72,6... | collective-permute-start | bytes 49160 | tf_op jit(solution)/shard_map/ppermute | solution.py:22
  126.6 6.7 %collective-permute-start.29 = (bf16[8,1,8,128]{3,2,0,1:T(8,128)(2,1)S(1)}, bf16[8,1,8,128]{3,2,0,1:T(8,128)(2,1)S(1)}, u32[]{:S(2)}, u32[]{:S(2)}) collective-permute-start(bf16[8,1,8,128]{3,2,0,1:T(8,128)(2,1)S(1)} %get-tuple-element.164), channel_id=1, source_target_pairs={{8,0},{16,8},{24,16},{32,24},{40,32},{48,40},{56,48},{64,56},{72,6... | collective-permute-start | bytes 49160 | tf_op jit(solution)/shard_map/ppermute | solution.py:22
  138.8 6.0 collective-permute-start.30
  147.8 5.1 collective-permute-done.31
  156.4 6.7 %collective-permute-start.17 = (bf16[8,1,8,128]{3,2,0,1:T(8,128)(2,1)S(1)}, bf16[8,1,8,128]{3,2,0,1:T(8,128)(2,1)S(1)}, u32[]{:S(2)}, u32[]{:S(2)}) collective-permute-start(bf16[8,1,8,128]{3,2,0,1:T(8,128)(2,1)S(1)} %get-tuple-element.154), channel_id=1, source_target_pairs={{8,0},{16,8},{24,16},{32,24},{40,32},{48,40},{56,48},{64,56},{72,6... | collective-permute-start | bytes 49160 | tf_op jit(solution)/shard_map/ppermute | solution.py:22
  165.2 6.7 %collective-permute-start.33 = (bf16[8,1,8,128]{3,2,0,1:T(8,128)(2,1)S(1)}, bf16[8,1,8,128]{3,2,0,1:T(8,128)(2,1)S(1)}, u32[]{:S(2)}, u32[]{:S(2)}) collective-permute-start(bf16[8,1,8,128]{3,2,0,1:T(8,128)(2,1)S(1)} %get-tuple-element.162), channel_id=1, source_target_pairs={{8,0},{16,8},{24,16},{32,24},{40,32},{48,40},{56,48},{64,56},{72,6... | collective-permute-start | bytes 49160 | tf_op jit(solution)/shard_map/ppermute | solution.py:22
  177.2 4.7 collective-permute-start.34
  185.4 10.4 %all-to-all-start = ((bf16[32,8,8,128]{3,2,0,1:T(8,128)(2,1)}), bf16[32,8,8,128]{3,2,0,1:T(8,128)(2,1)S(1)}, u32[]{:S(2)}, u32[]{:S(2)}) async-start(bf16[32,8,8,128]{3,2,0,1:T(8,128)(2,1)} %pad_maximum_fusion.1), calls=%async_computation | async-start | bytes 1048576 | tf_op jit(solution)/shard_map/all_to_all | solution.py:165
  198.2 5.9 all-to-all-done
  208.5 7.3 %all-to-all-done.1 = bf16[32,8,8,128]{3,2,0,1:T(8,128)(2,1)S(1)} async-done(((bf16[32,8,8,128]{3,2,0,1:T(8,128)(2,1)}), bf16[32,8,8,128]{3,2,0,1:T(8,128)(2,1)S(1)}, u32[]{:S(2)}, u32[]{:S(2)}) %all-to-all-start.1) | async-done | bytes 524320 | tf_op jit(solution)/shard_map/all_to_all | solution.py:165
  220.6 249.7 %all-reduce.23.cloned.1.call-done = f32[320,384]{1,0:T(8,128)} async-done(((f32[320,384]{1,0:T(8,128)}), f32[320,384]{1,0:T(8,128)}) %all-reduce.23.cloned.1.call-update) | async-done | bytes 491536 | tf_op jit(solution)/shard_map/psum | solution.py:183
  474.5 11.7 %cholesky.130 = f32[128,128]{1,0:T(8,128)S(1)} custom-call(f32[128,128]{1,0:T(8,128)S(1)} %cholesky.194), custom_call_target="Cholesky" | custom-call | tf_op jit(solution)/shard_map/jit(cholesky)/cholesky | solution.py:67
  486.9 9.8 %custom-call.13 = f32[1,128,128]{1,2,0:T(8,128)S(1)} custom-call(f32[1,128,128]{2,1,0:T(8,128)S(1)} %get-tuple-element.182), custom_call_target="InvertDiagBlocksLowerTriangular" | custom-call | tf_op jit(solution)/shard_map/jit(cholesky)/cholesky | solution.py:67
  497.2 11.9 %cholesky.147 = f32[128,128]{1,0:T(8,128)S(1)} custom-call(f32[128,128]{1,0:T(8,128)S(1)} %convolution_subtract_fusion.3), custom_call_target="Cholesky" | custom-call | tf_op jit(solution)/shard_map/jit(cholesky)/cholesky | solution.py:67
  511.3 4.1 while.4
  515.4 19.7 %custom-call.14 = f32[2,128,128]{1,2,0:T(8,128)S(1)} custom-call(f32[2,128,128]{2,1,0:T(8,128)S(1)} %get-tuple-element.19), custom_call_target="InvertDiagBlocksLowerTriangular" | custom-call | tf_op jit(solution)/shard_map/triangular_solve/custom-call.0 | solution.py:69
  542.5 11.7 %cholesky.164 = f32[128,128]{1,0:T(8,128)S(1)} custom-call(f32[128,128]{1,0:T(8,128)S(1)} %cholesky.197), custom_call_target="Cholesky" | custom-call | tf_op jit(solution)/shard_map/jit(cholesky)/cholesky | solution.py:67
  554.9 9.8 %custom-call.15 = f32[1,128,128]{1,2,0:T(8,128)S(1)} custom-call(f32[1,128,128]{2,1,0:T(8,128)S(1)} %get-tuple-element.178), custom_call_target="InvertDiagBlocksLowerTriangular" | custom-call | tf_op jit(solution)/shard_map/jit(cholesky)/cholesky | solution.py:67
  565.2 11.9 %cholesky.181 = f32[128,128]{1,0:T(8,128)S(1)} custom-call(f32[128,128]{1,0:T(8,128)S(1)} %convolution_subtract_fusion.2), custom_call_target="Cholesky" | custom-call | tf_op jit(solution)/shard_map/jit(cholesky)/cholesky | solution.py:67
  579.2 4.1 while.5
  583.4 19.7 %custom-call.16 = f32[2,128,128]{1,2,0:T(8,128)S(1)} custom-call(f32[2,128,128]{2,1,0:T(8,128)S(1)} %get-tuple-element.20), custom_call_target="InvertDiagBlocksLowerTriangular" | custom-call | tf_op jit(solution)/shard_map/triangular_solve/custom-call.0 | solution.py:69
  613.0 6.4 %copy.82 = bf16[8192,256]{1,0:T(8,128)(2,1)} copy(bf16[8192,256]{0,1:T(8,128)(2,1)} %fusion) | data formatting | bytes 8388608
  (274 shorter events, 120.0 us)
Async XLA Ops:
  9.1 34.6 %collective-permute-start = (bf16[1,8,128]{2,1,0:T(8,128)(2,1)}, bf16[1,8,128]{2,1,0:T(8,128)(2,1)}, u32[]{:S(2)}, u32[]{:S(2)}) collective-permute-start(bf16[1,8,128]{2,1,0:T(8,128)(2,1)} %get-tuple-element.185), channel_id=1, source_target_pairs={{0,8},{8,16},{16,24},{24,32},{32,40},{40,48},{48,56},{56,64},{64,7... | collective-permute-start | bytes 6152 | tf_op jit(solution)/shard_map/ppermute | solution.py:19
  11.1 32.7 %collective-permute-start.1 = (bf16[1,8,128]{2,1,0:T(8,128)(2,1)}, bf16[1,8,128]{2,1,0:T(8,128)(2,1)}, u32[]{:S(2)}, u32[]{:S(2)}) collective-permute-start(bf16[1,8,128]{2,1,0:T(8,128)(2,1)} %get-tuple-element.186), channel_id=1, source_target_pairs={{8,0},{16,8},{24,16},{32,24},{40,32},{48,40},{56,48},{64,56},{72,6... | collective-permute-start | bytes 6152 | tf_op jit(solution)/shard_map/ppermute | solution.py:22
  20.7 38.0 %collective-permute-start.4 = (bf16[8,1,8,128]{3,2,0,1:T(8,128)(2,1)}, bf16[8,1,8,128]{3,2,0,1:T(8,128)(2,1)S(1)}, u32[]{:S(2)}, u32[]{:S(2)}) collective-permute-start(bf16[8,1,8,128]{3,2,0,1:T(8,128)(2,1)} %get-tuple-element.159), channel_id=1, source_target_pairs={{0,8},{8,16},{16,24},{24,32},{32,40},{40,48},{48,56},{56,64},{64,7... | collective-permute-start | bytes 49160 | tf_op jit(solution)/shard_map/ppermute | solution.py:19
  22.6 36.1 %collective-permute-start.5 = (bf16[8,1,8,128]{3,2,0,1:T(8,128)(2,1)}, bf16[8,1,8,128]{3,2,0,1:T(8,128)(2,1)}, u32[]{:S(2)}, u32[]{:S(2)}) collective-permute-start(bf16[8,1,8,128]{3,2,0,1:T(8,128)(2,1)} %get-tuple-element.160), channel_id=1, source_target_pairs={{8,0},{16,8},{24,16},{32,24},{40,32},{48,40},{56,48},{64,56},{72,6... | collective-permute-start | bytes 49160 | tf_op jit(solution)/shard_map/ppermute | solution.py:22
  29.9 35.2 %collective-permute-start.20 = (bf16[8,1,8,128]{3,2,0,1:T(8,128)(2,1)}, bf16[8,1,8,128]{3,2,0,1:T(8,128)(2,1)S(1)}, u32[]{:S(2)}, u32[]{:S(2)}) collective-permute-start(bf16[8,1,8,128]{3,2,0,1:T(8,128)(2,1)} %get-tuple-element.167), channel_id=1, source_target_pairs={{0,8},{8,16},{16,24},{24,32},{32,40},{40,48},{48,56},{56,64},{64,7... | collective-permute-start | bytes 49160 | tf_op jit(solution)/shard_map/ppermute | solution.py:19
  48.1 9.4 %collective-permute-start.3 = (bf16[10,1,128]{2,1,0:T(2,128)(2,1)S(1)}, bf16[10,1,128]{2,1,0:T(2,128)(2,1)S(1)}, u32[]{:S(2)}, u32[]{:S(2)}) collective-permute-start(bf16[10,1,128]{2,1,0:T(2,128)(2,1)S(1)} %get-tuple-element.184), channel_id=1, source_target_pairs={{1,0},{2,1},{3,2},{4,3},{5,4},{6,5},{7,6},{9,8},{10,9},{11,10},{12... | collective-permute-start | bytes 7688 | tf_op jit(solution)/shard_map/ppermute | solution.py:22
  51.2 13.9 %collective-permute-start.21 = (bf16[8,1,8,128]{3,2,0,1:T(8,128)(2,1)}, bf16[8,1,8,128]{3,2,0,1:T(8,128)(2,1)S(1)}, u32[]{:S(2)}, u32[]{:S(2)}) collective-permute-start(bf16[8,1,8,128]{3,2,0,1:T(8,128)(2,1)} %get-tuple-element.168), channel_id=1, source_target_pairs={{8,0},{16,8},{24,16},{32,24},{40,32},{48,40},{56,48},{64,56},{72,6... | collective-permute-start | bytes 49160 | tf_op jit(solution)/shard_map/ppermute | solution.py:22
  59.5 11.5 %collective-permute-start.6 = (bf16[8,10,1,128]{3,2,0,1:T(2,128)(2,1)S(1)}, bf16[8,10,1,128]{3,2,0,1:T(2,128)(2,1)S(1)}, u32[]{:S(2)}, u32[]{:S(2)}) collective-permute-start(bf16[8,10,1,128]{3,2,0,1:T(2,128)(2,1)S(1)} %get-tuple-element.143), channel_id=1, source_target_pairs={{0,1},{1,2},{2,3},{3,4},{4,5},{5,6},{6,7},{8,9},{9,10},{10,11},{11... | collective-permute-start | bytes 61448 | tf_op jit(solution)/shard_map/ppermute | solution.py:19
  65.2 9.2 %collective-permute-start.22 = (bf16[8,10,1,128]{3,2,0,1:T(2,128)(2,1)S(1)}, bf16[8,10,1,128]{3,2,0,1:T(2,128)(2,1)S(1)}, u32[]{:S(2)}, u32[]{:S(2)}) collective-permute-start(bf16[8,10,1,128]{3,2,0,1:T(2,128)(2,1)S(1)} %get-tuple-element.151), channel_id=1, source_target_pairs={{0,1},{1,2},{2,3},{3,4},{4,5},{5,6},{6,7},{8,9},{9,10},{10,11},{11... | collective-permute-start | bytes 61448 | tf_op jit(solution)/shard_map/ppermute | solution.py:19
  77.2 17.5 %collective-permute-start.8 = (bf16[8,1,8,128]{3,2,0,1:T(8,128)(2,1)S(1)}, bf16[8,1,8,128]{3,2,0,1:T(8,128)(2,1)S(1)}, u32[]{:S(2)}, u32[]{:S(2)}) collective-permute-start(bf16[8,1,8,128]{3,2,0,1:T(8,128)(2,1)S(1)} %get-tuple-element.157), channel_id=1, source_target_pairs={{0,8},{8,16},{16,24},{24,32},{32,40},{40,48},{48,56},{56,64},{64,7... | collective-permute-start | bytes 49160 | tf_op jit(solution)/shard_map/ppermute | solution.py:19
  79.1 15.5 %collective-permute-start.9 = (bf16[8,1,8,128]{3,2,0,1:T(8,128)(2,1)S(1)}, bf16[8,1,8,128]{3,2,0,1:T(8,128)(2,1)S(1)}, u32[]{:S(2)}, u32[]{:S(2)}) collective-permute-start(bf16[8,1,8,128]{3,2,0,1:T(8,128)(2,1)S(1)} %get-tuple-element.158), channel_id=1, source_target_pairs={{8,0},{16,8},{24,16},{32,24},{40,32},{48,40},{56,48},{64,56},{72,6... | collective-permute-start | bytes 49160 | tf_op jit(solution)/shard_map/ppermute | solution.py:22
  85.9 13.6 %collective-permute-start.24 = (bf16[8,1,8,128]{3,2,0,1:T(8,128)(2,1)S(1)}, bf16[8,1,8,128]{3,2,0,1:T(8,128)(2,1)S(1)}, u32[]{:S(2)}, u32[]{:S(2)}) collective-permute-start(bf16[8,1,8,128]{3,2,0,1:T(8,128)(2,1)S(1)} %get-tuple-element.165), channel_id=1, source_target_pairs={{0,8},{8,16},{16,24},{24,32},{32,40},{40,48},{48,56},{56,64},{64,7... | collective-permute-start | bytes 49160 | tf_op jit(solution)/shard_map/ppermute | solution.py:19
  87.9 11.7 %collective-permute-start.25 = (bf16[8,1,8,128]{3,2,0,1:T(8,128)(2,1)S(1)}, bf16[8,1,8,128]{3,2,0,1:T(8,128)(2,1)S(1)}, u32[]{:S(2)}, u32[]{:S(2)}) collective-permute-start(bf16[8,1,8,128]{3,2,0,1:T(8,128)(2,1)S(1)} %get-tuple-element.166), channel_id=1, source_target_pairs={{8,0},{16,8},{24,16},{32,24},{40,32},{48,40},{56,48},{64,56},{72,6... | collective-permute-start | bytes 49160 | tf_op jit(solution)/shard_map/ppermute | solution.py:22
  94.7 13.1 %collective-permute-start.10 = (bf16[8,10,1,128]{3,2,0,1:T(2,128)(2,1)S(1)}, bf16[8,10,1,128]{3,2,0,1:T(2,128)(2,1)S(1)}, u32[]{:S(2)}, u32[]{:S(2)}) collective-permute-start(bf16[8,10,1,128]{3,2,0,1:T(2,128)(2,1)S(1)} %get-tuple-element.141), channel_id=1, source_target_pairs={{0,1},{1,2},{2,3},{3,4},{4,5},{5,6},{6,7},{8,9},{9,10},{10,11},{11... | collective-permute-start | bytes 61448 | tf_op jit(solution)/shard_map/ppermute | solution.py:19
  98.3 9.5 %collective-permute-start.11 = (bf16[8,10,1,128]{3,2,0,1:T(2,128)(2,1)S(1)}, bf16[8,10,1,128]{3,2,0,1:T(2,128)(2,1)S(1)}, u32[]{:S(2)}, u32[]{:S(2)}) collective-permute-start(bf16[8,10,1,128]{3,2,0,1:T(2,128)(2,1)S(1)} %get-tuple-element.142), channel_id=1, source_target_pairs={{1,0},{2,1},{3,2},{4,3},{5,4},{6,5},{7,6},{9,8},{10,9},{11,10},{12... | collective-permute-start | bytes 61448 | tf_op jit(solution)/shard_map/ppermute | solution.py:22
  99.7 9.8 %collective-permute-start.26 = (bf16[8,10,1,128]{3,2,0,1:T(2,128)(2,1)S(1)}, bf16[8,10,1,128]{3,2,0,1:T(2,128)(2,1)S(1)}, u32[]{:S(2)}, u32[]{:S(2)}) collective-permute-start(bf16[8,10,1,128]{3,2,0,1:T(2,128)(2,1)S(1)} %get-tuple-element.149), channel_id=1, source_target_pairs={{0,1},{1,2},{2,3},{3,4},{4,5},{5,6},{6,7},{8,9},{9,10},{10,11},{11... | collective-permute-start | bytes 61448 | tf_op jit(solution)/shard_map/ppermute | solution.py:19
  116.0 17.5 %collective-permute-start.12 = (bf16[8,1,8,128]{3,2,0,1:T(8,128)(2,1)S(1)}, bf16[8,1,8,128]{3,2,0,1:T(8,128)(2,1)S(1)}, u32[]{:S(2)}, u32[]{:S(2)}) collective-permute-start(bf16[8,1,8,128]{3,2,0,1:T(8,128)(2,1)S(1)} %get-tuple-element.155), channel_id=1, source_target_pairs={{0,8},{8,16},{16,24},{24,32},{32,40},{40,48},{48,56},{56,64},{64,7... | collective-permute-start | bytes 49160 | tf_op jit(solution)/shard_map/ppermute | solution.py:19
  117.9 15.5 %collective-permute-start.13 = (bf16[8,1,8,128]{3,2,0,1:T(8,128)(2,1)S(1)}, bf16[8,1,8,128]{3,2,0,1:T(8,128)(2,1)S(1)}, u32[]{:S(2)}, u32[]{:S(2)}) collective-permute-start(bf16[8,1,8,128]{3,2,0,1:T(8,128)(2,1)S(1)} %get-tuple-element.156), channel_id=1, source_target_pairs={{8,0},{16,8},{24,16},{32,24},{40,32},{48,40},{56,48},{64,56},{72,6... | collective-permute-start | bytes 49160 | tf_op jit(solution)/shard_map/ppermute | solution.py:22
  124.7 14.0 %collective-permute-start.28 = (bf16[8,1,8,128]{3,2,0,1:T(8,128)(2,1)S(1)}, bf16[8,1,8,128]{3,2,0,1:T(8,128)(2,1)S(1)}, u32[]{:S(2)}, u32[]{:S(2)}) collective-permute-start(bf16[8,1,8,128]{3,2,0,1:T(8,128)(2,1)S(1)} %get-tuple-element.163), channel_id=1, source_target_pairs={{0,8},{8,16},{16,24},{24,32},{32,40},{40,48},{48,56},{56,64},{64,7... | collective-permute-start | bytes 49160 | tf_op jit(solution)/shard_map/ppermute | solution.py:19
  126.6 12.1 %collective-permute-start.29 = (bf16[8,1,8,128]{3,2,0,1:T(8,128)(2,1)S(1)}, bf16[8,1,8,128]{3,2,0,1:T(8,128)(2,1)S(1)}, u32[]{:S(2)}, u32[]{:S(2)}) collective-permute-start(bf16[8,1,8,128]{3,2,0,1:T(8,128)(2,1)S(1)} %get-tuple-element.164), channel_id=1, source_target_pairs={{8,0},{16,8},{24,16},{32,24},{40,32},{48,40},{56,48},{64,56},{72,6... | collective-permute-start | bytes 49160 | tf_op jit(solution)/shard_map/ppermute | solution.py:22
  133.5 12.6 %collective-permute-start.14 = (bf16[8,10,1,128]{3,2,0,1:T(2,128)(2,1)S(1)}, bf16[8,10,1,128]{3,2,0,1:T(2,128)(2,1)S(1)}, u32[]{:S(2)}, u32[]{:S(2)}) collective-permute-start(bf16[8,10,1,128]{3,2,0,1:T(2,128)(2,1)S(1)} %get-tuple-element.139), channel_id=1, source_target_pairs={{0,1},{1,2},{2,3},{3,4},{4,5},{5,6},{6,7},{8,9},{9,10},{10,11},{11... | collective-permute-start | bytes 61448 | tf_op jit(solution)/shard_map/ppermute | solution.py:19
  138.8 9.0 %collective-permute-start.30 = (bf16[8,10,1,128]{3,2,0,1:T(2,128)(2,1)S(1)}, bf16[8,10,1,128]{3,2,0,1:T(2,128)(2,1)S(1)}, u32[]{:S(2)}, u32[]{:S(2)}) collective-permute-start(bf16[8,10,1,128]{3,2,0,1:T(2,128)(2,1)S(1)} %get-tuple-element.147), channel_id=1, source_target_pairs={{0,1},{1,2},{2,3},{3,4},{4,5},{5,6},{6,7},{8,9},{9,10},{10,11},{11... | collective-permute-start | bytes 61448 | tf_op jit(solution)/shard_map/ppermute | solution.py:19
  154.5 17.3 %collective-permute-start.16 = (bf16[8,1,8,128]{3,2,0,1:T(8,128)(2,1)S(1)}, bf16[8,1,8,128]{3,2,0,1:T(8,128)(2,1)S(1)}, u32[]{:S(2)}, u32[]{:S(2)}) collective-permute-start(bf16[8,1,8,128]{3,2,0,1:T(8,128)(2,1)S(1)} %get-tuple-element.153), channel_id=1, source_target_pairs={{0,8},{8,16},{16,24},{24,32},{32,40},{40,48},{48,56},{56,64},{64,7... | collective-permute-start | bytes 49160 | tf_op jit(solution)/shard_map/ppermute | solution.py:19
  156.4 15.4 %collective-permute-start.17 = (bf16[8,1,8,128]{3,2,0,1:T(8,128)(2,1)S(1)}, bf16[8,1,8,128]{3,2,0,1:T(8,128)(2,1)S(1)}, u32[]{:S(2)}, u32[]{:S(2)}) collective-permute-start(bf16[8,1,8,128]{3,2,0,1:T(8,128)(2,1)S(1)} %get-tuple-element.154), channel_id=1, source_target_pairs={{8,0},{16,8},{24,16},{32,24},{40,32},{48,40},{56,48},{64,56},{72,6... | collective-permute-start | bytes 49160 | tf_op jit(solution)/shard_map/ppermute | solution.py:22
  163.2 13.9 %collective-permute-start.32 = (bf16[8,1,8,128]{3,2,0,1:T(8,128)(2,1)S(1)}, bf16[8,1,8,128]{3,2,0,1:T(8,128)(2,1)S(1)}, u32[]{:S(2)}, u32[]{:S(2)}) collective-permute-start(bf16[8,1,8,128]{3,2,0,1:T(8,128)(2,1)S(1)} %get-tuple-element.161), channel_id=1, source_target_pairs={{0,8},{8,16},{16,24},{24,32},{32,40},{40,48},{48,56},{56,64},{64,7... | collective-permute-start | bytes 49160 | tf_op jit(solution)/shard_map/ppermute | solution.py:19
  165.2 12.0 %collective-permute-start.33 = (bf16[8,1,8,128]{3,2,0,1:T(8,128)(2,1)S(1)}, bf16[8,1,8,128]{3,2,0,1:T(8,128)(2,1)S(1)}, u32[]{:S(2)}, u32[]{:S(2)}) collective-permute-start(bf16[8,1,8,128]{3,2,0,1:T(8,128)(2,1)S(1)} %get-tuple-element.162), channel_id=1, source_target_pairs={{8,0},{16,8},{24,16},{32,24},{40,32},{48,40},{56,48},{64,56},{72,6... | collective-permute-start | bytes 49160 | tf_op jit(solution)/shard_map/ppermute | solution.py:22
  171.9 11.3 %collective-permute-start.18 = (bf16[8,10,1,128]{3,2,0,1:T(2,128)(2,1)S(1)}, bf16[8,10,1,128]{3,2,0,1:T(2,128)(2,1)S(1)}, u32[]{:S(2)}, u32[]{:S(2)}) collective-permute-start(bf16[8,10,1,128]{3,2,0,1:T(2,128)(2,1)S(1)} %get-tuple-element.137), channel_id=1, source_target_pairs={{0,1},{1,2},{2,3},{3,4},{4,5},{5,6},{6,7},{8,9},{9,10},{10,11},{11... | collective-permute-start | bytes 61448 | tf_op jit(solution)/shard_map/ppermute | solution.py:19
  177.2 18.7 %collective-permute-start.34 = (bf16[8,10,1,128]{3,2,0,1:T(2,128)(2,1)S(1)}, bf16[8,10,1,128]{3,2,0,1:T(2,128)(2,1)S(1)}, u32[]{:S(2)}, u32[]{:S(2)}) collective-permute-start(bf16[8,10,1,128]{3,2,0,1:T(2,128)(2,1)S(1)} %get-tuple-element.145), channel_id=1, source_target_pairs={{0,1},{1,2},{2,3},{3,4},{4,5},{5,6},{6,7},{8,9},{9,10},{10,11},{11... | collective-permute-start | bytes 61448 | tf_op jit(solution)/shard_map/ppermute | solution.py:19
  181.9 14.1 %collective-permute-start.35 = (bf16[8,10,1,128]{3,2,0,1:T(2,128)(2,1)S(1)}, bf16[8,10,1,128]{3,2,0,1:T(2,128)(2,1)S(1)}, u32[]{:S(2)}, u32[]{:S(2)}) collective-permute-start(bf16[8,10,1,128]{3,2,0,1:T(2,128)(2,1)S(1)} %get-tuple-element.146), channel_id=1, source_target_pairs={{1,0},{2,1},{3,2},{4,3},{5,4},{6,5},{7,6},{9,8},{10,9},{11,10},{12... | collective-permute-start | bytes 61448 | tf_op jit(solution)/shard_map/ppermute | solution.py:22
  185.4 18.6 %all-to-all-start = ((bf16[32,8,8,128]{3,2,0,1:T(8,128)(2,1)}), bf16[32,8,8,128]{3,2,0,1:T(8,128)(2,1)S(1)}, u32[]{:S(2)}, u32[]{:S(2)}) async-start(bf16[32,8,8,128]{3,2,0,1:T(8,128)(2,1)} %pad_maximum_fusion.1), calls=%async_computation | async-start | bytes 1048576 | tf_op jit(solution)/shard_map/all_to_all | solution.py:165
  204.1 11.7 %all-to-all-start.1 = ((bf16[32,8,8,128]{3,2,0,1:T(8,128)(2,1)}), bf16[32,8,8,128]{3,2,0,1:T(8,128)(2,1)S(1)}, u32[]{:S(2)}, u32[]{:S(2)}) async-start(bf16[32,8,8,128]{3,2,0,1:T(8,128)(2,1)} %pad_maximum_fusion.2), calls=%async_computation.1 | async-start | bytes 1048576 | tf_op jit(solution)/shard_map/all_to_all | solution.py:165
  207.6 262.7 %all-reduce.23.cloned.1.call-start = ((), (), s32[]{:S(2)}) async-start(), calls=%async_computation.2 | async-start | bytes 983040 | tf_op jit(solution)/shard_map/psum | solution.py:183
  (21 other events, 270.8 us)
Sparse Core Ops, SparseCore 0:
  219.8 250.5 all-reduce.22
where the time goes:
time: 635 us; the launch traced here: 627 us
  waiting for transfers between devices  274 us (43%)
  starting transfers between devices  145 us (23%)
  other arithmetic  131 us (21%)
  matrix products  30.2 us (5%)
  local copies, waits for them, and re-layouts  27.9 us (4%)
  between operations  18.7 us (3%)
    psum x1, waiting for transfers between devices, body(): whole = lax.psum(local, ('gx', 'sec')) / rows_total  250 us
    ppermute x18, starting transfers between devices, with_halo(): lax.ppermute(lax.slice_in_dim(block, 0, width, axis=dim), axis, backward)  72.6 us
    another operation x14, other arithmetic, batch_update(): factor = jnp.linalg.cholesky(inner)  69.7 us
    ppermute x18, starting transfers between devices, with_halo(): lax.ppermute(lax.slice_in_dim(block, block.shape[dim] - width, None, axis...  58.3 us
    another operation x5, other arithmetic, batch_update(): lax.linalg.triangular_solve(factor, eye, left_side=True, lower=True)  39.4 us
    all_to_all x2, starting transfers between devices, body(): lax.all_to_all(stacked, 'sec', split_axis=1, concat_axis=2, tiled=True)  13.9 us
    all_to_all x2, waiting for transfers between devices, body(): lax.all_to_all(stacked, 'sec', split_axis=1, concat_axis=2, tiled=True)  13.2 us
  transfers between devices with their start and end apart: 39, of which 6 were waited for; matrix products, arithmetic and copies ran while one was open for 5% of the time, Pallas kernels for 0%

commit v1 on v0

--- a/solution.py
+++ b/solution.py
@@ -180,7 +180,13 @@
         ],
         1,
     )
-    whole = lax.psum(local, ("gx", "sec")) / rows_total
+
+    def advance_strips_all_all(point):
+        for u in ("gx", "sec"):
+            point = lax.psum(point, u)
+        return point
+
+    whole = advance_strips_all_all(local) / rows_total
     w0, w1, w2, sigma = small_algebra(
         whole[:count, :count],
         whole[count:, :count],

time: 635 us -> 739 us (1.16)
  waiting for transfers between devices: 274 us -> 382 us
    psum x1 -> x2, waiting for transfers between devices: 250 us -> 356 us  [advance_strips_all_all(): point = lax.psum(point, u)]
  transfers between devices with their start and end apart: 39 -> 40, of which waited for: 6 -> 7; matrix products, arithmetic and copies ran while one was open for 5% -> 4% of each run, Pallas kernels for 0% -> 0%
where the time goes in v1:
time: 739 us; the launch traced here: 729 us
  waiting for transfers between devices  382 us (52%)
  starting transfers between devices  145 us (20%)
  other arithmetic  126 us (17%)
  matrix products  30.2 us (4%)
  local copies, waits for them, and re-layouts  26.3 us (4%)
  between operations  18.6 us (3%)
    psum x2, waiting for transfers between devices, advance_strips_all_all(): point = lax.psum(point, u)  356 us
    ppermute x18, starting transfers between devices, with_halo(): lax.ppermute(lax.slice_in_dim(block, 0, width, axis=dim), axis, backward)  72.5 us
    another operation x14, other arithmetic, batch_update(): factor = jnp.linalg.cholesky(inner)  69.6 us
    ppermute x18, starting transfers between devices, with_halo(): lax.ppermute(lax.slice_in_dim(block, block.shape[dim] - width, None, axis...  57.8 us
    another operation x5, other arithmetic, batch_update(): lax.linalg.triangular_solve(factor, eye, left_side=True, lower=True)  39.4 us
  transfers between devices with their start and end apart: 40, of which 7 were waited for; matrix products, arithmetic and copies ran while one was open for 4% of the time, Pallas kernels for 0%

profile of v1, /device:TPU:6, one launch (start us, length us, event | category | flops | bytes accessed | tf_op | source)
XLA Modules:
  0.0 728.5 jit_solution(16137149236737078778)
XLA Ops:
  10.5 7.9 %collective-permute-start.1 = (bf16[1,8,128]{2,1,0:T(8,128)(2,1)S(1)}, bf16[1,8,128]{2,1,0:T(8,128)(2,1)S(1)}, u32[]{:S(2)}, u32[]{:S(2)}) collective-permute-start(bf16[1,8,128]{2,1,0:T(8,128)(2,1)S(1)} %get-tuple-element.186), channel_id=1, source_target_pairs={{8,0},{16,8},{24,16},{32,24},{40,32},{48,40},{56,48},{64,56},{72,6... | collective-permute-start | bytes 6152 | tf_op jit(solution)/shard_map/ppermute | solution.py:22
  21.4 6.7 collective-permute-start.5
  32.8 5.5 fusion.8
  48.1 6.4 collective-permute-start.21
  54.9 4.3 collective-permute-start.6
  60.6 4.5 collective-permute-start.22
  74.5 6.7 collective-permute-start.9
  83.3 6.7 collective-permute-start.25
  95.1 6.7 collective-permute-start.26
  104.7 5.0 collective-permute-done.27
  113.5 6.7 collective-permute-start.13
  122.3 6.7 collective-permute-start.29
  134.5 5.3 collective-permute-start.30
  142.7 5.1 collective-permute-done.31
  151.4 6.7 collective-permute-start.17
  160.2 6.7 collective-permute-start.33
  172.2 4.7 collective-permute-start.34
  180.4 10.4 %all-to-all-start = ((bf16[32,8,8,128]{3,2,0,1:T(8,128)(2,1)}), bf16[32,8,8,128]{3,2,0,1:T(8,128)(2,1)S(1)}, u32[]{:S(2)}, u32[]{:S(2)}) async-start(bf16[32,8,8,128]{3,2,0,1:T(8,128)(2,1)} %pad_maximum_fusion.1), calls=%async_computation | async-start | bytes 1048576 | tf_op jit(solution)/shard_map/all_to_all | solution.py:165
  193.1 5.9 all-to-all-done
  203.0 7.7 %all-to-all-done.1 = bf16[32,8,8,128]{3,2,0,1:T(8,128)(2,1)S(1)} async-done(((bf16[32,8,8,128]{3,2,0,1:T(8,128)(2,1)}), bf16[32,8,8,128]{3,2,0,1:T(8,128)(2,1)S(1)}, u32[]{:S(2)}, u32[]{:S(2)}) %all-to-all-start.1) | async-done | bytes 524320 | tf_op jit(solution)/shard_map/all_to_all | solution.py:165
  215.1 264.8 %all-reduce.24.cloned.1.call-done = f32[320,384]{1,0:T(8,128)} async-done(((f32[320,384]{1,0:T(8,128)}), f32[320,384]{1,0:T(8,128)}) %all-reduce.24.cloned.1.call-update) | async-done | bytes 491536 | tf_op jit(solution)/shard_map/psum | solution.py:186
  480.9 91.5 %all-reduce.26.cloned.1.call-done = f32[320,384]{1,0:T(8,128)} async-done(((f32[320,384]{1,0:T(8,128)}), f32[320,384]{1,0:T(8,128)}) %all-reduce.26.cloned.1.call-update) | async-done | bytes 491536 | tf_op jit(solution)/shard_map/psum | solution.py:186
  576.6 11.7 %cholesky.130 = f32[128,128]{1,0:T(8,128)S(1)} custom-call(f32[128,128]{1,0:T(8,128)S(1)} %cholesky.194), custom_call_target="Cholesky" | custom-call | tf_op jit(solution)/shard_map/jit(cholesky)/cholesky | solution.py:67
  589.0 9.8 %custom-call.13 = f32[1,128,128]{1,2,0:T(8,128)S(1)} custom-call(f32[1,128,128]{2,1,0:T(8,128)S(1)} %get-tuple-element.182), custom_call_target="InvertDiagBlocksLowerTriangular" | custom-call | tf_op jit(solution)/shard_map/jit(cholesky)/cholesky | solution.py:67
  599.3 11.9 %cholesky.147 = f32[128,128]{1,0:T(8,128)S(1)} custom-call(f32[128,128]{1,0:T(8,128)S(1)} %convolution_subtract_fusion.3), custom_call_target="Cholesky" | custom-call | tf_op jit(solution)/shard_map/jit(cholesky)/cholesky | solution.py:67
  617.1 19.7 %custom-call.14 = f32[2,128,128]{1,2,0:T(8,128)S(1)} custom-call(f32[2,128,128]{2,1,0:T(8,128)S(1)} %get-tuple-element.19), custom_call_target="InvertDiagBlocksLowerTriangular" | custom-call | tf_op jit(solution)/shard_map/triangular_solve/custom-call.0 | solution.py:69
  644.1 11.7 %cholesky.164 = f32[128,128]{1,0:T(8,128)S(1)} custom-call(f32[128,128]{1,0:T(8,128)S(1)} %cholesky.197), custom_call_target="Cholesky" | custom-call | tf_op jit(solution)/shard_map/jit(cholesky)/cholesky | solution.py:67
  656.5 9.8 %custom-call.15 = f32[1,128,128]{1,2,0:T(8,128)S(1)} custom-call(f32[1,128,128]{2,1,0:T(8,128)S(1)} %get-tuple-element.178), custom_call_target="InvertDiagBlocksLowerTriangular" | custom-call | tf_op jit(solution)/shard_map/jit(cholesky)/cholesky | solution.py:67
  666.8 11.9 %cholesky.181 = f32[128,128]{1,0:T(8,128)S(1)} custom-call(f32[128,128]{1,0:T(8,128)S(1)} %convolution_subtract_fusion.2), custom_call_target="Cholesky" | custom-call | tf_op jit(solution)/shard_map/jit(cholesky)/cholesky | solution.py:67
  680.8 4.0 while.5
  684.8 19.7 %custom-call.16 = f32[2,128,128]{1,2,0:T(8,128)S(1)} custom-call(f32[2,128,128]{2,1,0:T(8,128)S(1)} %get-tuple-element.20), custom_call_target="InvertDiagBlocksLowerTriangular" | custom-call | tf_op jit(solution)/shard_map/triangular_solve/custom-call.0 | solution.py:69
  714.4 6.4 copy.82
  (269 shorter events, 118.9 us)
Async XLA Ops:
  8.6 33.4 %collective-permute-start = (bf16[1,8,128]{2,1,0:T(8,128)(2,1)S(1)}, bf16[1,8,128]{2,1,0:T(8,128)(2,1)S(1)}, u32[]{:S(2)}, u32[]{:S(2)}) collective-permute-start(bf16[1,8,128]{2,1,0:T(8,128)(2,1)S(1)} %get-tuple-element.185), channel_id=1, source_target_pairs={{0,8},{8,16},{16,24},{24,32},{32,40},{40,48},{48,56},{56,64},{64,7... | collective-permute-start | bytes 6152 | tf_op jit(solution)/shard_map/ppermute | solution.py:19
  10.5 31.5 %collective-permute-start.1 = (bf16[1,8,128]{2,1,0:T(8,128)(2,1)S(1)}, bf16[1,8,128]{2,1,0:T(8,128)(2,1)S(1)}, u32[]{:S(2)}, u32[]{:S(2)}) collective-permute-start(bf16[1,8,128]{2,1,0:T(8,128)(2,1)S(1)} %get-tuple-element.186), channel_id=1, source_target_pairs={{8,0},{16,8},{24,16},{32,24},{40,32},{48,40},{56,48},{64,56},{72,6... | collective-permute-start | bytes 6152 | tf_op jit(solution)/shard_map/ppermute | solution.py:22
  19.5 35.4 %collective-permute-start.4 = (bf16[8,1,8,128]{3,2,0,1:T(8,128)(2,1)S(1)}, bf16[8,1,8,128]{3,2,0,1:T(8,128)(2,1)S(1)}, u32[]{:S(2)}, u32[]{:S(2)}) collective-permute-start(bf16[8,1,8,128]{3,2,0,1:T(8,128)(2,1)S(1)} %get-tuple-element.159), channel_id=1, source_target_pairs={{0,8},{8,16},{16,24},{24,32},{32,40},{40,48},{48,56},{56,64},{64,7... | collective-permute-start | bytes 49160 | tf_op jit(solution)/shard_map/ppermute | solution.py:19
  21.4 33.4 %collective-permute-start.5 = (bf16[8,1,8,128]{3,2,0,1:T(8,128)(2,1)S(1)}, bf16[8,1,8,128]{3,2,0,1:T(8,128)(2,1)S(1)}, u32[]{:S(2)}, u32[]{:S(2)}) collective-permute-start(bf16[8,1,8,128]{3,2,0,1:T(8,128)(2,1)S(1)} %get-tuple-element.160), channel_id=1, source_target_pairs={{8,0},{16,8},{24,16},{32,24},{40,32},{48,40},{56,48},{64,56},{72,6... | collective-permute-start | bytes 49160 | tf_op jit(solution)/shard_map/ppermute | solution.py:22
  28.1 32.4 %collective-permute-start.20 = (bf16[8,1,8,128]{3,2,0,1:T(8,128)(2,1)S(1)}, bf16[8,1,8,128]{3,2,0,1:T(8,128)(2,1)S(1)}, u32[]{:S(2)}, u32[]{:S(2)}) collective-permute-start(bf16[8,1,8,128]{3,2,0,1:T(8,128)(2,1)S(1)} %get-tuple-element.167), channel_id=1, source_target_pairs={{0,8},{8,16},{16,24},{24,32},{32,40},{40,48},{48,56},{56,64},{64,7... | collective-permute-start | bytes 49160 | tf_op jit(solution)/shard_map/ppermute | solution.py:19
  45.6 8.9 %collective-permute-start.3 = (bf16[10,1,128]{2,1,0:T(2,128)(2,1)S(1)}, bf16[10,1,128]{2,1,0:T(2,128)(2,1)S(1)}, u32[]{:S(2)}, u32[]{:S(2)}) collective-permute-start(bf16[10,1,128]{2,1,0:T(2,128)(2,1)S(1)} %get-tuple-element.184), channel_id=1, source_target_pairs={{1,0},{2,1},{3,2},{4,3},{5,4},{6,5},{7,6},{9,8},{10,9},{11,10},{12... | collective-permute-start | bytes 7688 | tf_op jit(solution)/shard_map/ppermute | solution.py:22
  48.1 12.4 %collective-permute-start.21 = (bf16[8,1,8,128]{3,2,0,1:T(8,128)(2,1)S(1)}, bf16[8,1,8,128]{3,2,0,1:T(8,128)(2,1)S(1)}, u32[]{:S(2)}, u32[]{:S(2)}) collective-permute-start(bf16[8,1,8,128]{3,2,0,1:T(8,128)(2,1)S(1)} %get-tuple-element.168), channel_id=1, source_target_pairs={{8,0},{16,8},{24,16},{32,24},{40,32},{48,40},{56,48},{64,56},{72,6... | collective-permute-start | bytes 49160 | tf_op jit(solution)/shard_map/ppermute | solution.py:22
  54.9 11.5 %collective-permute-start.6 = (bf16[8,10,1,128]{3,2,0,1:T(2,128)(2,1)S(1)}, bf16[8,10,1,128]{3,2,0,1:T(2,128)(2,1)S(1)}, u32[]{:S(2)}, u32[]{:S(2)}) collective-permute-start(bf16[8,10,1,128]{3,2,0,1:T(2,128)(2,1)S(1)} %get-tuple-element.143), channel_id=1, source_target_pairs={{0,1},{1,2},{2,3},{3,4},{4,5},{5,6},{6,7},{8,9},{9,10},{10,11},{11... | collective-permute-start | bytes 61448 | tf_op jit(solution)/shard_map/ppermute | solution.py:19
  60.6 8.4 %collective-permute-start.22 = (bf16[8,10,1,128]{3,2,0,1:T(2,128)(2,1)S(1)}, bf16[8,10,1,128]{3,2,0,1:T(2,128)(2,1)S(1)}, u32[]{:S(2)}, u32[]{:S(2)}) collective-permute-start(bf16[8,10,1,128]{3,2,0,1:T(2,128)(2,1)S(1)} %get-tuple-element.151), channel_id=1, source_target_pairs={{0,1},{1,2},{2,3},{3,4},{4,5},{5,6},{6,7},{8,9},{9,10},{10,11},{11... | collective-permute-start | bytes 61448 | tf_op jit(solution)/shard_map/ppermute | solution.py:19
  72.6 17.5 %collective-permute-start.8 = (bf16[8,1,8,128]{3,2,0,1:T(8,128)(2,1)S(1)}, bf16[8,1,8,128]{3,2,0,1:T(8,128)(2,1)S(1)}, u32[]{:S(2)}, u32[]{:S(2)}) collective-permute-start(bf16[8,1,8,128]{3,2,0,1:T(8,128)(2,1)S(1)} %get-tuple-element.157), channel_id=1, source_target_pairs={{0,8},{8,16},{16,24},{24,32},{32,40},{40,48},{48,56},{56,64},{64,7... | collective-permute-start | bytes 49160 | tf_op jit(solution)/shard_map/ppermute | solution.py:19
  74.5 15.5 %collective-permute-start.9 = (bf16[8,1,8,128]{3,2,0,1:T(8,128)(2,1)S(1)}, bf16[8,1,8,128]{3,2,0,1:T(8,128)(2,1)S(1)}, u32[]{:S(2)}, u32[]{:S(2)}) collective-permute-start(bf16[8,1,8,128]{3,2,0,1:T(8,128)(2,1)S(1)} %get-tuple-element.158), channel_id=1, source_target_pairs={{8,0},{16,8},{24,16},{32,24},{40,32},{48,40},{56,48},{64,56},{72,6... | collective-permute-start | bytes 49160 | tf_op jit(solution)/shard_map/ppermute | solution.py:22
  81.3 13.6 %collective-permute-start.24 = (bf16[8,1,8,128]{3,2,0,1:T(8,128)(2,1)S(1)}, bf16[8,1,8,128]{3,2,0,1:T(8,128)(2,1)S(1)}, u32[]{:S(2)}, u32[]{:S(2)}) collective-permute-start(bf16[8,1,8,128]{3,2,0,1:T(8,128)(2,1)S(1)} %get-tuple-element.165), channel_id=1, source_target_pairs={{0,8},{8,16},{16,24},{24,32},{32,40},{40,48},{48,56},{56,64},{64,7... | collective-permute-start | bytes 49160 | tf_op jit(solution)/shard_map/ppermute | solution.py:19
  83.3 11.7 %collective-permute-start.25 = (bf16[8,1,8,128]{3,2,0,1:T(8,128)(2,1)S(1)}, bf16[8,1,8,128]{3,2,0,1:T(8,128)(2,1)S(1)}, u32[]{:S(2)}, u32[]{:S(2)}) collective-permute-start(bf16[8,1,8,128]{3,2,0,1:T(8,128)(2,1)S(1)} %get-tuple-element.166), channel_id=1, source_target_pairs={{8,0},{16,8},{24,16},{32,24},{40,32},{48,40},{56,48},{64,56},{72,6... | collective-permute-start | bytes 49160 | tf_op jit(solution)/shard_map/ppermute | solution.py:22
  90.1 12.9 %collective-permute-start.10 = (bf16[8,10,1,128]{3,2,0,1:T(2,128)(2,1)S(1)}, bf16[8,10,1,128]{3,2,0,1:T(2,128)(2,1)S(1)}, u32[]{:S(2)}, u32[]{:S(2)}) collective-permute-start(bf16[8,10,1,128]{3,2,0,1:T(2,128)(2,1)S(1)} %get-tuple-element.141), channel_id=1, source_target_pairs={{0,1},{1,2},{2,3},{3,4},{4,5},{5,6},{6,7},{8,9},{9,10},{10,11},{11... | collective-permute-start | bytes 61448 | tf_op jit(solution)/shard_map/ppermute | solution.py:19
  93.7 9.4 %collective-permute-start.11 = (bf16[8,10,1,128]{3,2,0,1:T(2,128)(2,1)S(1)}, bf16[8,10,1,128]{3,2,0,1:T(2,128)(2,1)S(1)}, u32[]{:S(2)}, u32[]{:S(2)}) collective-permute-start(bf16[8,10,1,128]{3,2,0,1:T(2,128)(2,1)S(1)} %get-tuple-element.142), channel_id=1, source_target_pairs={{1,0},{2,1},{3,2},{4,3},{5,4},{6,5},{7,6},{9,8},{10,9},{11,10},{12... | collective-permute-start | bytes 61448 | tf_op jit(solution)/shard_map/ppermute | solution.py:22
  95.1 9.6 %collective-permute-start.26 = (bf16[8,10,1,128]{3,2,0,1:T(2,128)(2,1)S(1)}, bf16[8,10,1,128]{3,2,0,1:T(2,128)(2,1)S(1)}, u32[]{:S(2)}, u32[]{:S(2)}) collective-permute-start(bf16[8,10,1,128]{3,2,0,1:T(2,128)(2,1)S(1)} %get-tuple-element.149), channel_id=1, source_target_pairs={{0,1},{1,2},{2,3},{3,4},{4,5},{5,6},{6,7},{8,9},{9,10},{10,11},{11... | collective-permute-start | bytes 61448 | tf_op jit(solution)/shard_map/ppermute | solution.py:19
  111.4 17.7 %collective-permute-start.12 = (bf16[8,1,8,128]{3,2,0,1:T(8,128)(2,1)S(1)}, bf16[8,1,8,128]{3,2,0,1:T(8,128)(2,1)S(1)}, u32[]{:S(2)}, u32[]{:S(2)}) collective-permute-start(bf16[8,1,8,128]{3,2,0,1:T(8,128)(2,1)S(1)} %get-tuple-element.155), channel_id=1, source_target_pairs={{0,8},{8,16},{16,24},{24,32},{32,40},{40,48},{48,56},{56,64},{64,7... | collective-permute-start | bytes 49160 | tf_op jit(solution)/shard_map/ppermute | solution.py:19
  113.5 15.5 %collective-permute-start.13 = (bf16[8,1,8,128]{3,2,0,1:T(8,128)(2,1)S(1)}, bf16[8,1,8,128]{3,2,0,1:T(8,128)(2,1)S(1)}, u32[]{:S(2)}, u32[]{:S(2)}) collective-permute-start(bf16[8,1,8,128]{3,2,0,1:T(8,128)(2,1)S(1)} %get-tuple-element.156), channel_id=1, source_target_pairs={{8,0},{16,8},{24,16},{32,24},{40,32},{48,40},{56,48},{64,56},{72,6... | collective-permute-start | bytes 49160 | tf_op jit(solution)/shard_map/ppermute | solution.py:22
  120.3 14.0 %collective-permute-start.28 = (bf16[8,1,8,128]{3,2,0,1:T(8,128)(2,1)S(1)}, bf16[8,1,8,128]{3,2,0,1:T(8,128)(2,1)S(1)}, u32[]{:S(2)}, u32[]{:S(2)}) collective-permute-start(bf16[8,1,8,128]{3,2,0,1:T(8,128)(2,1)S(1)} %get-tuple-element.163), channel_id=1, source_target_pairs={{0,8},{8,16},{16,24},{24,32},{32,40},{40,48},{48,56},{56,64},{64,7... | collective-permute-start | bytes 49160 | tf_op jit(solution)/shard_map/ppermute | solution.py:19
  122.3 12.1 %collective-permute-start.29 = (bf16[8,1,8,128]{3,2,0,1:T(8,128)(2,1)S(1)}, bf16[8,1,8,128]{3,2,0,1:T(8,128)(2,1)S(1)}, u32[]{:S(2)}, u32[]{:S(2)}) collective-permute-start(bf16[8,1,8,128]{3,2,0,1:T(8,128)(2,1)S(1)} %get-tuple-element.164), channel_id=1, source_target_pairs={{8,0},{16,8},{24,16},{32,24},{40,32},{48,40},{56,48},{64,56},{72,6... | collective-permute-start | bytes 49160 | tf_op jit(solution)/shard_map/ppermute | solution.py:22
  129.1 11.9 %collective-permute-start.14 = (bf16[8,10,1,128]{3,2,0,1:T(2,128)(2,1)S(1)}, bf16[8,10,1,128]{3,2,0,1:T(2,128)(2,1)S(1)}, u32[]{:S(2)}, u32[]{:S(2)}) collective-permute-start(bf16[8,10,1,128]{3,2,0,1:T(2,128)(2,1)S(1)} %get-tuple-element.139), channel_id=1, source_target_pairs={{0,1},{1,2},{2,3},{3,4},{4,5},{5,6},{6,7},{8,9},{9,10},{10,11},{11... | collective-permute-start | bytes 61448 | tf_op jit(solution)/shard_map/ppermute | solution.py:19
  149.5 17.3 %collective-permute-start.16 = (bf16[8,1,8,128]{3,2,0,1:T(8,128)(2,1)S(1)}, bf16[8,1,8,128]{3,2,0,1:T(8,128)(2,1)S(1)}, u32[]{:S(2)}, u32[]{:S(2)}) collective-permute-start(bf16[8,1,8,128]{3,2,0,1:T(8,128)(2,1)S(1)} %get-tuple-element.153), channel_id=1, source_target_pairs={{0,8},{8,16},{16,24},{24,32},{32,40},{40,48},{48,56},{56,64},{64,7... | collective-permute-start | bytes 49160 | tf_op jit(solution)/shard_map/ppermute | solution.py:19
  151.4 15.4 %collective-permute-start.17 = (bf16[8,1,8,128]{3,2,0,1:T(8,128)(2,1)S(1)}, bf16[8,1,8,128]{3,2,0,1:T(8,128)(2,1)S(1)}, u32[]{:S(2)}, u32[]{:S(2)}) collective-permute-start(bf16[8,1,8,128]{3,2,0,1:T(8,128)(2,1)S(1)} %get-tuple-element.154), channel_id=1, source_target_pairs={{8,0},{16,8},{24,16},{32,24},{40,32},{48,40},{56,48},{64,56},{72,6... | collective-permute-start | bytes 49160 | tf_op jit(solution)/shard_map/ppermute | solution.py:22
  158.2 13.9 %collective-permute-start.32 = (bf16[8,1,8,128]{3,2,0,1:T(8,128)(2,1)S(1)}, bf16[8,1,8,128]{3,2,0,1:T(8,128)(2,1)S(1)}, u32[]{:S(2)}, u32[]{:S(2)}) collective-permute-start(bf16[8,1,8,128]{3,2,0,1:T(8,128)(2,1)S(1)} %get-tuple-element.161), channel_id=1, source_target_pairs={{0,8},{8,16},{16,24},{24,32},{32,40},{40,48},{48,56},{56,64},{64,7... | collective-permute-start | bytes 49160 | tf_op jit(solution)/shard_map/ppermute | solution.py:19
  160.2 12.0 %collective-permute-start.33 = (bf16[8,1,8,128]{3,2,0,1:T(8,128)(2,1)S(1)}, bf16[8,1,8,128]{3,2,0,1:T(8,128)(2,1)S(1)}, u32[]{:S(2)}, u32[]{:S(2)}) collective-permute-start(bf16[8,1,8,128]{3,2,0,1:T(8,128)(2,1)S(1)} %get-tuple-element.162), channel_id=1, source_target_pairs={{8,0},{16,8},{24,16},{32,24},{40,32},{48,40},{56,48},{64,56},{72,6... | collective-permute-start | bytes 49160 | tf_op jit(solution)/shard_map/ppermute | solution.py:22
  166.9 11.3 %collective-permute-start.18 = (bf16[8,10,1,128]{3,2,0,1:T(2,128)(2,1)S(1)}, bf16[8,10,1,128]{3,2,0,1:T(2,128)(2,1)S(1)}, u32[]{:S(2)}, u32[]{:S(2)}) collective-permute-start(bf16[8,10,1,128]{3,2,0,1:T(2,128)(2,1)S(1)} %get-tuple-element.137), channel_id=1, source_target_pairs={{0,1},{1,2},{2,3},{3,4},{4,5},{5,6},{6,7},{8,9},{9,10},{10,11},{11... | collective-permute-start | bytes 61448 | tf_op jit(solution)/shard_map/ppermute | solution.py:19
  172.2 18.7 %collective-permute-start.34 = (bf16[8,10,1,128]{3,2,0,1:T(2,128)(2,1)S(1)}, bf16[8,10,1,128]{3,2,0,1:T(2,128)(2,1)S(1)}, u32[]{:S(2)}, u32[]{:S(2)}) collective-permute-start(bf16[8,10,1,128]{3,2,0,1:T(2,128)(2,1)S(1)} %get-tuple-element.145), channel_id=1, source_target_pairs={{0,1},{1,2},{2,3},{3,4},{4,5},{5,6},{6,7},{8,9},{9,10},{10,11},{11... | collective-permute-start | bytes 61448 | tf_op jit(solution)/shard_map/ppermute | solution.py:19
  176.9 14.0 %collective-permute-start.35 = (bf16[8,10,1,128]{3,2,0,1:T(2,128)(2,1)S(1)}, bf16[8,10,1,128]{3,2,0,1:T(2,128)(2,1)S(1)}, u32[]{:S(2)}, u32[]{:S(2)}) collective-permute-start(bf16[8,10,1,128]{3,2,0,1:T(2,128)(2,1)S(1)} %get-tuple-element.146), channel_id=1, source_target_pairs={{1,0},{2,1},{3,2},{4,3},{5,4},{6,5},{7,6},{9,8},{10,9},{11,10},{12... | collective-permute-start | bytes 61448 | tf_op jit(solution)/shard_map/ppermute | solution.py:22
  180.4 18.6 %all-to-all-start = ((bf16[32,8,8,128]{3,2,0,1:T(8,128)(2,1)}), bf16[32,8,8,128]{3,2,0,1:T(8,128)(2,1)S(1)}, u32[]{:S(2)}, u32[]{:S(2)}) async-start(bf16[32,8,8,128]{3,2,0,1:T(8,128)(2,1)} %pad_maximum_fusion.1), calls=%async_computation | async-start | bytes 1048576 | tf_op jit(solution)/shard_map/all_to_all | solution.py:165
  199.0 11.7 %all-to-all-start.1 = ((bf16[32,8,8,128]{3,2,0,1:T(8,128)(2,1)}), bf16[32,8,8,128]{3,2,0,1:T(8,128)(2,1)S(1)}, u32[]{:S(2)}, u32[]{:S(2)}) async-start(bf16[32,8,8,128]{3,2,0,1:T(8,128)(2,1)} %pad_maximum_fusion.2), calls=%async_computation.1 | async-start | bytes 1048576 | tf_op jit(solution)/shard_map/all_to_all | solution.py:165
  202.5 277.4 %all-reduce.24.cloned.1.call-start = ((), (), s32[]{:S(2)}) async-start(), calls=%async_computation.2 | async-start | bytes 983040 | tf_op jit(solution)/shard_map/psum | solution.py:186
  214.6 357.8 %all-reduce.26.cloned.1.call-start = ((), (), s32[]{:S(2)}) async-start(), calls=%async_computation.3 | async-start | bytes 983040 | tf_op jit(solution)/shard_map/psum | solution.py:186
  (18 other events, 466.0 us)
Sparse Core Ops, SparseCore 0:
  214.7 265.1 all-reduce.23
  482.6 89.7 all-reduce.25
